TPU v7x, 32 devices: a whole 2x2x4 slice. The times are simulated.
32 devices in a mesh: rows: 8 (over z, y), cols: 2 (over x), dp: 2 (over core).
Axes of the slice: x: 2, y: 2, z: 4, core: 2. Of those that a mesh axis runs over, the one named last changes fastest.
Arguments:
- queries: bfloat16 [2, 128, 32, 1024], P('dp', 'rows', 'cols'), may hold values from -69 to 69
- keys_values: bfloat16 [2, 2, 128, 32, 1024], P(None, 'dp', 'rows', 'cols'), may hold values from -6 to 6
- out_weight: bfloat16 [1024, 1024], replicated, may hold values from -0.1875 to 0.1875
- out_grad: bfloat16 [2, 128, 32, 1024], P('dp', 'rows', 'cols'), may hold values from -6 to 6
Outputs:
- attn_out: bfloat16 [2, 128, 32, 1024], P('dp', 'rows', 'cols')
- query_grad: bfloat16 [2, 128, 32, 1024], P('dp', 'rows', 'cols')
- kv_grad: bfloat16 [2, 2, 128, 32, 1024], P(None, 'dp', 'rows', 'cols')
- weight_grad: float32 [1024, 1024], P('rows', ('cols', 'dp'))
All inputs are finite; a program needn't handle non-finite values.
Results may differ from a plain program's by a relative error of at most 0.012.
The roundings to bfloat16 on the way count: a program that leaves them out, or rounds other values in their place, can miss the bound.
Values may be sent and summed in bfloat16 or wider, within the bound.
A program may use at most 128 MiB of HBM per device.

v0:
```python
import functools
import math

import jax
import jax.numpy as jnp
from jax import lax
from jax.experimental import pallas as pl
from jax.experimental.pallas import tpu as pltpu
from jax.sharding import PartitionSpec as P

NH = 16
HD = 64
RAD = 6
WIN = 13
QB = 8
PAIR = 2 * HD
GROUP = QB * RAD
MESH = pl.DeviceIdType.MESH
F32 = jnp.float32
BF16 = jnp.bfloat16


def mm(a, b, ca, cb):
    return lax.dot_general(a, b, (((ca,), (cb,)), ((), ())), preferred_element_type=F32)


def kernel(
    tile_h, tile_w, n_rows, n_cols, n_dp,
    q_ref, kv_ref, w_ref, og_ref,
    out_ref, dq_ref, kvg_ref, wg_ref,
    main, strip, sstrip, acc, sacc, bias, probs, att_t, d_att,
    rim_out, rim_in, srim_out, srim_in,
    slab, slab_low, got_dp, low_cols, got_cols, low_rows, got_rows,
    halo_send, halo_recv, rim_send, rim_recv, sum_send, sum_recv,
):
    sides = strip.shape[0]
    blocks = tile_h // QB
    tokens = tile_h * tile_w
    width = q_ref.shape[1]
    pairs = width // PAIR
    edge = RAD * tile_w
    span = (QB + 2 * RAD) * tile_w
    sspan = 3 * GROUP
    step = QB * tile_w
    image_h, image_w = tile_h * n_rows, tile_w * n_cols
    scale = 1.0 / math.sqrt(HD)
    r, c, d = lax.axis_index("rows"), lax.axis_index("cols"), lax.axis_index("dp")

    links = [(-1, None), (1, None)] + [(dr, s) for s in range(sides) for dr in (0, -1, 1)]

    def partner(dr, s):
        if s is None:
            col = c
        elif sides == 1:
            col = 1 - c
        else:
            col = c + (2 * s - 1)
        return {"rows": r + dr, "cols": col}

    def there(dr, s):
        ok = None
        if dr:
            ok = r > 0 if dr < 0 else r < n_rows - 1
        if s is not None and sides == 2:
            side_ok = c > 0 if s == 0 else c < n_cols - 1
            ok = side_ok if ok is None else ok & side_ok
        return ok

    def guarded(dr, s, action):
        ok = there(dr, s)
        if ok is None:
            action()
        else:
            pl.when(ok)(action)

    def slot(s):
        return 0 if sides == 1 else 1 - s

    def starts_at(s):
        if sides == 1:
            return (1 - c) * (tile_w - RAD)
        return 0 if s == 0 else tile_w - RAD

    barrier = pltpu.get_barrier_semaphore()
    for k in range(1, n_rows):
        pl.semaphore_signal(barrier, 1, device_id={"rows": lax.rem(r + k, n_rows)}, device_id_type=MESH)
    for k in range(1, n_cols):
        pl.semaphore_signal(barrier, 1, device_id={"cols": lax.rem(c + k, n_cols)}, device_id_type=MESH)
    for k in range(1, n_dp):
        pl.semaphore_signal(barrier, 1, device_id={"dp": lax.rem(d + k, n_dp)}, device_id_type=MESH)
    greeted = n_rows + n_cols + n_dp - 3
    for dr, s in links:
        if dr and s is not None:
            def greet(dr=dr, s=s):
                pl.semaphore_signal(barrier, 1, device_id=partner(dr, s), device_id_type=MESH)
            guarded(dr, s, greet)
            greeted = greeted + there(dr, s).astype(jnp.int32)

    strip_tokens = tile_h * RAD

    def pick(n, s):
        token = lax.broadcasted_iota(jnp.int32, (n, tokens), 0)
        row = (token * 10923) >> 16
        col = token - row * RAD
        place = row * tile_w + col + starts_at(s)
        return (place == lax.broadcasted_iota(jnp.int32, (n, tokens), 1)).astype(F32).astype(BF16)

    def scatter(s):
        shape = (tokens, GROUP * (blocks + 2))
        token = lax.broadcasted_iota(jnp.int32, shape, 1)
        row = (token * 10923) >> 16
        col = token - row * RAD
        row = row - jnp.where(row < QB, 0, jnp.where(row < QB + tile_h, QB, 2 * QB))
        place = row * tile_w + col + starts_at(s)
        return (place == lax.broadcasted_iota(jnp.int32, shape, 0)).astype(F32).astype(BF16)

    for s in range(sides):
        chosen = pick(strip_tokens, s)
        for k in range(2):
            sstrip[s, k] = mm(chosen, kv_ref[k], 1, 0).astype(BF16)

    pl.semaphore_wait(barrier, greeted)

    def halo_copy(index):
        dr, s = links[index]
        if s is None:
            if dr < 0:
                src, dst = kv_ref.at[:, pl.ds(0, edge)], main.at[:, pl.ds(edge + tokens, edge)]
            else:
                src, dst = kv_ref.at[:, pl.ds(tokens - edge, edge)], main.at[:, pl.ds(0, edge)]
        else:
            own, far = sstrip.at[s], strip.at[slot(s)]
            if dr == 0:
                src, dst = own, far.at[:, pl.ds(GROUP, strip_tokens)]
            elif dr < 0:
                src, dst = own.at[:, pl.ds(0, GROUP)], far.at[:, pl.ds(GROUP + strip_tokens, GROUP)]
            else:
                src, dst = own.at[:, pl.ds(strip_tokens - GROUP, GROUP)], far.at[:, pl.ds(0, GROUP)]
        return src, dst

    def rim_copy(index):
        dr, s = links[index]
        if s is None:
            at = 0 if dr < 0 else 1
            return rim_out.at[at], rim_in.at[1 - at]
        own, far = srim_out.at[s], srim_in.at[slot(s)]
        if dr == 0:
            return own.at[:, pl.ds(GROUP, strip_tokens)], far.at[:, pl.ds(GROUP, strip_tokens)]
        if dr < 0:
            return own.at[:, pl.ds(0, GROUP)], far.at[:, pl.ds(GROUP + strip_tokens, GROUP)]
        return own.at[:, pl.ds(GROUP + strip_tokens, GROUP)], far.at[:, pl.ds(0, GROUP)]

    def mirror(index):
        dr, s = links[index]
        return links.index((-dr, None if s is None else (s if sides == 1 else 1 - s)))

    def remote(copy, index, send, recv):
        src, dst = copy(index)
        return pltpu.make_async_remote_copy(
            src_ref=src, dst_ref=dst, send_sem=send.at[index], recv_sem=recv.at[mirror(index)],
            device_id=partner(*links[index]), device_id_type=MESH,
        )

    def start_all(copy, send, recv):
        for index in range(len(links)):
            guarded(*links[index], lambda index=index: remote(copy, index, send, recv).start())

    def wait_all(copy, send, recv):
        for index in range(len(links)):
            def action(index=index):
                src, dst = copy(mirror(index))
                pltpu.make_async_remote_copy(
                    src_ref=src, dst_ref=dst, send_sem=send.at[index], recv_sem=recv.at[index],
                    device_id=partner(*links[index]), device_id_type=MESH,
                ).wait_recv()
                remote(copy, index, send, recv).wait_send()
            guarded(*links[index], action)

    start_all(halo_copy, halo_send, halo_recv)

    for index in range(len(links)):
        ok = there(*links[index])
        if ok is not None:
            def clear(index=index):
                dst = halo_copy(mirror(index))[1]
                dst[...] = jnp.zeros(dst.shape, BF16)
                dst = rim_copy(mirror(index))[1]
                dst[...] = jnp.zeros(dst.shape, BF16)
            pl.when(jnp.logical_not(ok))(clear)

    for k in range(2):
        main[k, edge : edge + tokens] = kv_ref[k]

    d_att[...] = mm(og_ref[...], w_ref[...], 1, 1).astype(BF16)
    acc[...] = jnp.zeros(acc.shape, F32)
    sacc[...] = jnp.zeros(sacc.shape, F32)

    def put_bias(b, at, rows, cols, n):
        lane = lax.broadcasted_iota(jnp.int32, (n, step), 1)
        q_row = r * tile_h + b * QB + lane // tile_w
        q_col = c * tile_w + lane % tile_w
        first_r = jnp.clip(q_row - RAD, 0, image_h - WIN)
        first_c = jnp.clip(q_col - RAD, 0, image_w - WIN)
        ok = (rows >= first_r) & (rows < first_r + WIN) & (cols >= first_c) & (cols < first_c + WIN)
        bias[b, at : at + n] = jnp.where(ok, 0.0, -1e30)

    for b in range(blocks):
        token = lax.broadcasted_iota(jnp.int32, (span, step), 0)
        put_bias(b, 0, r * tile_h + b * QB - RAD + token // tile_w, c * tile_w + token % tile_w, span)
        token = lax.broadcasted_iota(jnp.int32, (sspan, step), 0)
        row = (token * 10923) >> 16
        for s in range(sides):
            if sides == 1:
                first = c * tile_w + jnp.where(c == 0, tile_w, -RAD)
            else:
                first = c * tile_w + (tile_w if s else -RAD)
            put_bias(
                b, span + s * sspan, r * tile_h + (b - 1) * QB + row, first + token - row * RAD, sspan
            )

    wait_all(halo_copy, halo_send, halo_recv)

    def lanes(p):
        return pl.ds(pl.multiple_of(p * PAIR, PAIR), PAIR)

    def keys_of(k, b, p):
        parts = [main[k, step * b : step * b + span, lanes(p)]]
        for s in range(sides):
            parts.append(strip[s, k, GROUP * b : GROUP * b + sspan, lanes(p)])
        return jnp.concatenate(parts, axis=0)

    def split_heads(x):
        low_head = lax.broadcasted_iota(jnp.int32, x.shape, 1) < HD
        wide = x.astype(F32)
        return jnp.concatenate(
            [jnp.where(low_head, wide, 0.0), jnp.where(low_head, 0.0, wide)], axis=0
        ).astype(BF16)

    def queries_of(b, p):
        return split_heads(q_ref[step * b : step * (b + 1), lanes(p)].astype(F32) * scale)

    def scores_of(keys, b, p):
        hidden = bias[b]
        return mm(keys, queries_of(b, p), 1, 1) + jnp.concatenate([hidden, hidden], axis=1)

    keep = probs.shape[1] == span + sides * sspan

    def own_heads(x):
        return jnp.concatenate([x[:HD, :step], x[HD:, step:]], axis=0)

    for b in range(blocks):
        def forward(p, carry, b=b):
            keys, values = keys_of(0, b, p), keys_of(1, b, p)
            scores = scores_of(keys, b, p)
            top = jnp.max(scores, axis=0, keepdims=True)
            expd = jnp.exp(scores - top)
            share = 1.0 / jnp.sum(expd, axis=0, keepdims=True)
            full = expd * share
            if keep:
                probs[b * pairs + p] = full
            else:
                probs[b * pairs + p, 0:1] = top
                probs[b * pairs + p, 1:2] = share
            att = own_heads(mm(values, full.astype(BF16), 0, 0)).astype(BF16)
            att_t[pl.ds(pl.multiple_of(p * PAIR, PAIR), PAIR), step * b : step * (b + 1)] = att
            return carry

        lax.fori_loop(0, pairs, forward, 0)

    block_c = slab.shape[3]
    rows_c = width // n_rows
    og = og_ref[...]
    for j in range(n_cols):
        for e in range(n_dp):
            at = (j * n_dp + e) * block_c
            product = mm(att_t[...], og[:, at : at + block_c], 1, 0)
            slab[e, j] = product
            slab_low[e, j] = product.astype(BF16)

    def dp_copy(k):
        to = lax.rem(d + k, n_dp)
        return pltpu.make_async_remote_copy(
            src_ref=slab_low.at[to], dst_ref=got_dp.at[k - 1],
            send_sem=sum_send.at[0, k - 1], recv_sem=sum_recv.at[0, k - 1],
            device_id={"dp": to}, device_id_type=MESH,
        )

    def cols_copy(k):
        to = lax.rem(c + k, n_cols)
        return pltpu.make_async_remote_copy(
            src_ref=low_cols.at[to], dst_ref=got_cols.at[k - 1],
            send_sem=sum_send.at[1, k - 1], recv_sem=sum_recv.at[1, k - 1],
            device_id={"cols": to}, device_id_type=MESH,
        )

    def rows_copy(k):
        to = lax.rem(r + k, n_rows)
        return pltpu.make_async_remote_copy(
            src_ref=low_rows.at[to], dst_ref=got_rows.at[k - 1],
            send_sem=sum_send.at[2, k - 1], recv_sem=sum_recv.at[2, k - 1],
            device_id={"rows": to}, device_id_type=MESH,
        )

    for k in range(1, n_dp):
        dp_copy(k).start()
    out_ref[...] = mm(att_t[...], w_ref[...], 0, 0).astype(BF16)

    for b in range(blocks):
        def backward(p, carry, b=b):
            keys, values = keys_of(0, b, p), keys_of(1, b, p)
            d_blk = d_att[step * b : step * (b + 1), lanes(p)]
            d_two = split_heads(d_blk)
            att = att_t[pl.ds(pl.multiple_of(p * PAIR, PAIR), PAIR), step * b : step * (b + 1)]
            both = d_blk.astype(F32).T * att.astype(F32)
            delta = jnp.concatenate(
                [
                    jnp.sum(both[:HD], axis=0, keepdims=True),
                    jnp.sum(both[HD:], axis=0, keepdims=True),
                ],
                axis=1,
            )
            if keep:
                full = probs[b * pairs + p]
            else:
                top, share = probs[b * pairs + p, 0:1], probs[b * pairs + p, 1:2]
                full = jnp.exp(scores_of(keys, b, p) - top) * share
            dscores = (full * (mm(values, d_two, 1, 1) - delta)).astype(BF16)
            dq = own_heads(mm(keys, dscores, 0, 0)) * scale
            dq_ref[step * b : step * (b + 1), lanes(p)] = dq.T.astype(BF16)
            for k, grad in (
                (0, mm(dscores, queries_of(b, p), 1, 0)),
                (1, mm(full.astype(BF16), d_two, 1, 0)),
            ):
                acc[k, step * b : step * b + span, lanes(p)] += grad[:span]
                for s in range(sides):
                    at = span + s * sspan
                    sacc[s, k, GROUP * b : GROUP * b + sspan, lanes(p)] += grad[at : at + sspan]
            return carry

        lax.fori_loop(0, pairs, backward, 0)
        if b == 0:
            for k in range(1, n_dp):
                dp_copy(k).wait()
            for j in range(n_cols):
                total = slab[d, j]
                for k in range(1, n_dp):
                    total = total + got_dp[k - 1, j].astype(F32)
                slab[d, j] = total
                low_cols[j] = total.astype(BF16)
            for k in range(1, n_cols):
                cols_copy(k).start()

    for k in range(2):
        rim_out[0, k] = acc[k, :edge].astype(BF16)
        rim_out[1, k] = acc[k, edge + tokens :].astype(BF16)
        for s in range(sides):
            srim_out[s, k] = sacc[s, k].astype(BF16)
    start_all(rim_copy, rim_send, rim_recv)

    for k in range(1, n_cols):
        cols_copy(k).wait()
    total = slab[d, c]
    for k in range(1, n_cols):
        total = total + got_cols[k - 1].astype(F32)
    slab[d, c] = total
    for i in range(n_rows):
        low_rows[i] = total[i * rows_c : (i + 1) * rows_c].astype(BF16)
    for k in range(1, n_rows):
        rows_copy(k).start()

    wait_all(rim_copy, rim_send, rim_recv)
    for k in range(2):
        own = acc[k, edge : edge + tokens]
        for s in range(sides):
            own = own + mm(scatter(s), srim_in[s, k], 1, 0)
        acc[k, edge : edge + tokens] = own
        acc[k, edge : 2 * edge] += rim_in[0, k].astype(F32)
        acc[k, tokens : edge + tokens] += rim_in[1, k].astype(F32)
        kvg_ref[k] = acc[k, edge : edge + tokens].astype(BF16)

    for k in range(1, n_rows):
        rows_copy(k).wait()
    total = slab[d, c, pl.ds(pl.multiple_of(r * rows_c, rows_c), rows_c)]
    for k in range(1, n_rows):
        total = total + got_rows[k - 1].astype(F32)
    wg_ref[...] = total * (1.0 / math.sqrt(image_h * image_w * n_dp))


def local(n_rows, n_cols, n_dp, queries, keys_values, out_weight, out_grad):
    tile_h, tile_w, width = queries.shape[1:]
    tokens = tile_h * tile_w
    sides = 1 if n_cols == 2 else 2
    blocks = tile_h // QB
    pairs = width // PAIR
    edge = RAD * tile_w
    grown = tokens + 2 * edge
    sgrown = GROUP * (blocks + 2)
    seen = (QB + 2 * RAD) * tile_w + sides * 3 * GROUP
    step = QB * tile_w
    keep = blocks * pairs * seen * 2 * step * 4 < 12 * 2**20
    block_c = width // (n_cols * n_dp)
    rows_c = width // n_rows
    links = 2 + 3 * sides
    most = max(n_rows, n_cols, n_dp) - 1
    vmem = pl.BlockSpec(memory_space=pltpu.VMEM)
    dma = pltpu.SemaphoreType.DMA
    out, dq, kvg, wg = pl.pallas_call(
        functools.partial(kernel, tile_h, tile_w, n_rows, n_cols, n_dp),
        out_shape=(
            jax.ShapeDtypeStruct((tokens, width), BF16),
            jax.ShapeDtypeStruct((tokens, width), BF16),
            jax.ShapeDtypeStruct((2, tokens, width), BF16),
            jax.ShapeDtypeStruct((rows_c, block_c), F32),
        ),
        in_specs=[vmem] * 4,
        out_specs=(vmem,) * 4,
        scratch_shapes=[
            pltpu.VMEM((2, grown, width), BF16),
            pltpu.VMEM((sides, 2, sgrown, width), BF16),
            pltpu.VMEM((sides, 2, tile_h * RAD, width), BF16),
            pltpu.VMEM((2, grown, width), F32),
            pltpu.VMEM((sides, 2, sgrown, width), F32),
            pltpu.VMEM((blocks, seen, step), F32),
            pltpu.VMEM((blocks * pairs, seen if keep else 8, 2 * step), F32),
            pltpu.VMEM((width, tokens), BF16),
            pltpu.VMEM((tokens, width), BF16),
            pltpu.VMEM((2, 2, edge, width), BF16),
            pltpu.VMEM((2, 2, edge, width), BF16),
            pltpu.VMEM((sides, 2, sgrown, width), BF16),
            pltpu.VMEM((sides, 2, sgrown, width), BF16),
            pltpu.VMEM((n_dp, n_cols, width, block_c), F32),
            pltpu.VMEM((n_dp, n_cols, width, block_c), BF16),
            pltpu.VMEM((n_dp - 1, n_cols, width, block_c), BF16),
            pltpu.VMEM((n_cols, width, block_c), BF16),
            pltpu.VMEM((n_cols - 1, width, block_c), BF16),
            pltpu.VMEM((n_rows, rows_c, block_c), BF16),
            pltpu.VMEM((n_rows - 1, rows_c, block_c), BF16),
            dma((links,)), dma((links,)), dma((links,)), dma((links,)),
            dma((3, most)), dma((3, most)),
        ],
        compiler_params=pltpu.CompilerParams(
            collective_id=0, has_side_effects=True, vmem_limit_bytes=60 * 2**20
        ),
    )(
        queries.reshape(tokens, width),
        keys_values.reshape(2, tokens, width),
        out_weight,
        out_grad.reshape(tokens, width),
    )
    return (
        out.reshape(queries.shape),
        dq.reshape(queries.shape),
        kvg.reshape(keys_values.shape),
        wg,
    )


def solution(mesh):
    in_specs = (
        P("dp", "rows", "cols", None),
        P(None, "dp", "rows", "cols", None),
        P(),
        P("dp", "rows", "cols", None),
    )
    out_specs = (
        P("dp", "rows", "cols", None),
        P("dp", "rows", "cols", None),
        P(None, "dp", "rows", "cols", None),
        P("rows", ("cols", "dp")),
    )
    sizes = (mesh.shape["rows"], mesh.shape["cols"], mesh.shape["dp"])
    return jax.shard_map(
        functools.partial(local, *sizes),
        mesh=mesh, in_specs=in_specs, out_specs=out_specs, check_vma=False,
    )
```

profile of v0, /device:TPU:8, one launch (start us, length us, event | category | flops | bytes accessed | tf_op | source)
XLA Modules:
  0.0 94.8 jit_solution(4835020032129336315)
XLA Ops:
  0.6 88.6 %shard_map.75 = (bf16[256,1024]{1,0:T(8,128)(2,1)}, bf16[256,1024]{1,0:T(8,128)(2,1)}, bf16[2,256,1024]{2,1,0:T(8,128)(2,1)}, f32[128,256]{1,0:T(8,128)}) custom-call(bf16[256,1024]{1,0:T(8,128)(2,1)} %bitcast.12, bf16[2,256,1024]{2,1,0:T(8,128)(2,1)} %bitcast.9, bf16[1024,1024]{1,0:T(8,128)(2,1)} %w_ref.1, bf16[256,1024]{1,0:T(8,128)(2,1)} %bitcast.13), custom_call_target="tpu_custom_call" | custom-call | tf_op jit(solution)/shard_map/pallas_call | solution.py:407
  89.3 0.0 copy-start
  89.3 0.0 copy-start.1
  89.3 2.0 %copy.13 = bf16[1,16,16,1024]{3,2,1,0:T(8,128)(2,1)} copy(bf16[1,16,16,1024]{3,2,1,0:T(8,128)(2,1)} %bitcast.11) | data formatting | bytes 1048576
  91.3 1.9 %copy.14 = bf16[1,16,16,1024]{3,2,1,0:T(8,128)(2,1)} copy(bf16[1,16,16,1024]{3,2,1,0:T(8,128)(2,1)} %bitcast.10) | data formatting | bytes 1048576
  93.1 0.0 copy-done
  93.1 1.0 %copy.15 = bf16[2,1,16,16,1024]{4,3,2,1,0:T(8,128)(2,1)} copy(bf16[2,1,16,16,1024]{4,3,2,1,0:T(8,128)(2,1)S(1)} %bitcast.8) | data formatting | bytes 2097152
  94.1 0.0 copy-done.1
  94.1 0.7 copy.16
Async XLA Ops:
  89.3 3.9 %copy-start = (bf16[2,256,1024]{2,1,0:T(8,128)(2,1)S(1)}, bf16[2,256,1024]{2,1,0:T(8,128)(2,1)}, u32[]{:S(2)}) copy-start(bf16[2,256,1024]{2,1,0:T(8,128)(2,1)} %get-tuple-element.10) | copy-start | bytes 3145732
  89.3 4.8 %copy-start.1 = (f32[128,256]{1,0:T(8,128)S(1)}, f32[128,256]{1,0:T(8,128)}, u32[]{:S(2)}) copy-start(f32[128,256]{1,0:T(8,128)} %get-tuple-element.23) | copy-start | bytes 393220
where the time goes:
time: 95 us; the launch traced here: 94.8 us
  Pallas kernels  88.6 us (93%)
  local copies, waits for them, and re-layouts  5.49 us (6%)
    pallas_call x1, Pallas kernels, local(): pl.pallas_call(functools.partial(kernel, tile_h, tile_w, n_rows, n_cols,...  88.6 us
    unnamed x8, local copies, waits for them, and re-layouts  5.49 us

commit v1 on v0

v1 whole, which is shorter than its diff:
```python
import functools
import math

import jax
import jax.numpy as jnp
from jax import lax
from jax.experimental import pallas as pl
from jax.experimental.pallas import tpu as pltpu
from jax.sharding import PartitionSpec as P

NH = 16
HD = 64
RAD = 6
WIN = 13
QB = 8
PAIR = 2 * HD
CHUNK = 2
GROUP = QB * RAD
MESH = pl.DeviceIdType.MESH
F32 = jnp.float32
BF16 = jnp.bfloat16


def mm(a, b, ca, cb):
    return lax.dot_general(a, b, (((ca,), (cb,)), ((), ())), preferred_element_type=F32)


def kernel(
    tile_h, tile_w, n_rows, n_cols, n_dp,
    q_ref, kv_ref, w_ref, og_ref,
    out_ref, dq_ref, kvg_ref, wg_ref,
    main, strip, sstrip, acc, sacc, bias, att_t, d_att,
    rim_out, rim_in, srim_out, srim_in,
    slab, slab_low, got_dp, low_cols, got_cols, low_rows, got_rows,
    halo_send, halo_recv, rim_send, rim_recv, dp_sems, cols_sems, rows_sems,
):
    sides = strip.shape[0]
    blocks = tile_h // QB
    tokens = tile_h * tile_w
    width = q_ref.shape[1]
    pairs = width // PAIR
    edge = RAD * tile_w
    span = (QB + 2 * RAD) * tile_w
    sspan = 3 * GROUP
    step = QB * tile_w
    image_h, image_w = tile_h * n_rows, tile_w * n_cols
    scale = 1.0 / math.sqrt(HD)
    r, c, d = lax.axis_index("rows"), lax.axis_index("cols"), lax.axis_index("dp")

    links = [(-1, None), (1, None)] + [(dr, s) for s in range(sides) for dr in (0, -1, 1)]

    def partner(dr, s):
        if s is None:
            col = c
        elif sides == 1:
            col = 1 - c
        else:
            col = c + (2 * s - 1)
        return {"rows": r + dr, "cols": col}

    def there(dr, s):
        ok = None
        if dr:
            ok = r > 0 if dr < 0 else r < n_rows - 1
        if s is not None and sides == 2:
            side_ok = c > 0 if s == 0 else c < n_cols - 1
            ok = side_ok if ok is None else ok & side_ok
        return ok

    def guarded(dr, s, action):
        ok = there(dr, s)
        if ok is None:
            action()
        else:
            pl.when(ok)(action)

    def slot(s):
        return 0 if sides == 1 else 1 - s

    def starts_at(s):
        if sides == 1:
            return (1 - c) * (tile_w - RAD)
        return 0 if s == 0 else tile_w - RAD

    barrier = pltpu.get_barrier_semaphore()
    for k in range(1, n_rows):
        pl.semaphore_signal(barrier, 1, device_id={"rows": lax.rem(r + k, n_rows)}, device_id_type=MESH)
    for k in range(1, n_cols):
        pl.semaphore_signal(barrier, 1, device_id={"cols": lax.rem(c + k, n_cols)}, device_id_type=MESH)
    for k in range(1, n_dp):
        pl.semaphore_signal(barrier, 1, device_id={"dp": lax.rem(d + k, n_dp)}, device_id_type=MESH)
    greeted = n_rows + n_cols + n_dp - 3
    for dr, s in links:
        if dr and s is not None:
            def greet(dr=dr, s=s):
                pl.semaphore_signal(barrier, 1, device_id=partner(dr, s), device_id_type=MESH)
            guarded(dr, s, greet)
            greeted = greeted + there(dr, s).astype(jnp.int32)

    strip_tokens = tile_h * RAD

    def pick(n, s):
        token = lax.broadcasted_iota(jnp.int32, (n, tokens), 0)
        row = (token * 10923) >> 16
        col = token - row * RAD
        place = row * tile_w + col + starts_at(s)
        return (place == lax.broadcasted_iota(jnp.int32, (n, tokens), 1)).astype(F32).astype(BF16)

    def scatter(s):
        shape = (tokens, GROUP * (blocks + 2))
        token = lax.broadcasted_iota(jnp.int32, shape, 1)
        row = (token * 10923) >> 16
        col = token - row * RAD
        row = row - jnp.where(row < QB, 0, jnp.where(row < QB + tile_h, QB, 2 * QB))
        place = row * tile_w + col + starts_at(s)
        return (place == lax.broadcasted_iota(jnp.int32, shape, 0)).astype(F32).astype(BF16)

    for s in range(sides):
        chosen = pick(strip_tokens, s)
        for k in range(2):
            sstrip[s, k] = mm(chosen, kv_ref[k], 1, 0).astype(BF16)

    pl.semaphore_wait(barrier, greeted)

    chunks = pairs // CHUNK
    part = CHUNK * PAIR

    def halo_copy(index, at):
        dr, s = links[index]
        if s is None:
            if dr < 0:
                return kv_ref.at[:, pl.ds(0, edge), at], main.at[:, pl.ds(edge + tokens, edge), at]
            return kv_ref.at[:, pl.ds(tokens - edge, edge), at], main.at[:, pl.ds(0, edge), at]
        own, far = sstrip.at[s], strip.at[slot(s)]
        if dr == 0:
            return own.at[:, :, at], far.at[:, pl.ds(GROUP, strip_tokens), at]
        if dr < 0:
            return own.at[:, pl.ds(0, GROUP), at], far.at[:, pl.ds(GROUP + strip_tokens, GROUP), at]
        return own.at[:, pl.ds(strip_tokens - GROUP, GROUP), at], far.at[:, pl.ds(0, GROUP), at]

    def rim_copy(index, at):
        dr, s = links[index]
        if s is None:
            way = 0 if dr < 0 else 1
            return rim_out.at[way, :, :, at], rim_in.at[1 - way, :, :, at]
        own, far = srim_out.at[s], srim_in.at[slot(s)]
        if dr == 0:
            which = pl.ds(GROUP, strip_tokens)
            return own.at[:, which, at], far.at[:, which, at]
        first, last = pl.ds(0, GROUP), pl.ds(GROUP + strip_tokens, GROUP)
        if dr < 0:
            return own.at[:, first, at], far.at[:, last, at]
        return own.at[:, last, at], far.at[:, first, at]

    def mirror(index):
        dr, s = links[index]
        return links.index((-dr, None if s is None else (s if sides == 1 else 1 - s)))

    def remote(copy, index, g, send, recv):
        src, dst = copy(index, pl.ds(g * part, part))
        return pltpu.make_async_remote_copy(
            src_ref=src, dst_ref=dst, send_sem=send.at[index, g], recv_sem=recv.at[mirror(index), g],
            device_id=partner(*links[index]), device_id_type=MESH,
        )

    def start_all(copy, g, send, recv):
        for index in range(len(links)):
            guarded(*links[index], lambda index=index: remote(copy, index, g, send, recv).start())

    def wait_all(copy, g, send, recv):
        for index in range(len(links)):
            def action(index=index):
                src, dst = copy(mirror(index), pl.ds(g * part, part))
                pltpu.make_async_remote_copy(
                    src_ref=src, dst_ref=dst, send_sem=send.at[index, g], recv_sem=recv.at[index, g],
                    device_id=partner(*links[index]), device_id_type=MESH,
                ).wait_recv()
                remote(copy, index, g, send, recv).wait_send()
            guarded(*links[index], action)

    for g in range(chunks):
        start_all(halo_copy, g, halo_send, halo_recv)

    for index in range(len(links)):
        ok = there(*links[index])
        if ok is not None:
            def clear(index=index):
                dst = halo_copy(mirror(index), pl.ds(0, width))[1]
                dst[...] = jnp.zeros(dst.shape, BF16)
                dst = rim_copy(mirror(index), pl.ds(0, width))[1]
                dst[...] = jnp.zeros(dst.shape, BF16)
            pl.when(jnp.logical_not(ok))(clear)

    for k in range(2):
        main[k, edge : edge + tokens] = kv_ref[k]
    got_rows[r] = jnp.zeros(got_rows.shape[1:], BF16)

    d_att[...] = mm(og_ref[...], w_ref[...], 1, 1).astype(BF16)
    acc[...] = jnp.zeros(acc.shape, F32)
    sacc[...] = jnp.zeros(sacc.shape, F32)

    def put_bias(b, at, rows, cols, n):
        lane = lax.broadcasted_iota(jnp.int32, (n, step), 1)
        q_row = r * tile_h + b * QB + lane // tile_w
        q_col = c * tile_w + lane % tile_w
        first_r = jnp.clip(q_row - RAD, 0, image_h - WIN)
        first_c = jnp.clip(q_col - RAD, 0, image_w - WIN)
        ok = (rows >= first_r) & (rows < first_r + WIN) & (cols >= first_c) & (cols < first_c + WIN)
        bias[b, at : at + n] = jnp.where(ok, 0.0, -1e30)

    for b in range(blocks):
        token = lax.broadcasted_iota(jnp.int32, (span, step), 0)
        put_bias(b, 0, r * tile_h + b * QB - RAD + token // tile_w, c * tile_w + token % tile_w, span)
        token = lax.broadcasted_iota(jnp.int32, (sspan, step), 0)
        row = (token * 10923) >> 16
        for s in range(sides):
            if sides == 1:
                first = c * tile_w + jnp.where(c == 0, tile_w, -RAD)
            else:
                first = c * tile_w + (tile_w if s else -RAD)
            put_bias(
                b, span + s * sspan, r * tile_h + (b - 1) * QB + row, first + token - row * RAD, sspan
            )

    def lanes(p):
        return pl.ds(pl.multiple_of(p * PAIR, PAIR), PAIR)

    def keys_of(k, b, p):
        parts = [main[k, step * b : step * b + span, lanes(p)]]
        for s in range(sides):
            parts.append(strip[s, k, GROUP * b : GROUP * b + sspan, lanes(p)])
        return jnp.concatenate(parts, axis=0)

    def split_heads(x):
        low_head = lax.broadcasted_iota(jnp.int32, x.shape, 1) < HD
        wide = x.astype(F32)
        return jnp.concatenate(
            [jnp.where(low_head, wide, 0.0), jnp.where(low_head, 0.0, wide)], axis=0
        ).astype(BF16)

    def queries_of(b, p):
        return split_heads(q_ref[step * b : step * (b + 1), lanes(p)].astype(F32) * scale)

    def own_heads(x):
        return jnp.concatenate([x[:HD, :step], x[HD:, step:]], axis=0)

    def attend(p, carry):
        for b in range(blocks):
            here = slice(step * b, step * (b + 1))
            keys, values = keys_of(0, b, p), keys_of(1, b, p)
            q_two = queries_of(b, p)
            d_blk = d_att[here, lanes(p)]
            d_two = split_heads(d_blk)
            hidden = bias[b]
            scores = mm(keys, q_two, 1, 1) + jnp.concatenate([hidden, hidden], axis=1)
            expd = jnp.exp(scores - jnp.max(scores, axis=0, keepdims=True))
            full = expd * (1.0 / jnp.sum(expd, axis=0, keepdims=True))
            low = full.astype(BF16)
            att = own_heads(mm(values, low, 0, 0)).astype(BF16)
            att_t[lanes(p), here] = att
            both = d_blk.astype(F32).T * att.astype(F32)
            delta = jnp.concatenate(
                [
                    jnp.sum(both[:HD], axis=0, keepdims=True),
                    jnp.sum(both[HD:], axis=0, keepdims=True),
                ],
                axis=1,
            )
            dscores = (full * (mm(values, d_two, 1, 1) - delta)).astype(BF16)
            dq = own_heads(mm(keys, dscores, 0, 0)) * scale
            dq_ref[here, lanes(p)] = dq.T.astype(BF16)
            for k, grad in ((0, mm(dscores, q_two, 1, 0)), (1, mm(low, d_two, 1, 0))):
                acc[k, step * b : step * b + span, lanes(p)] += grad[:span]
                for s in range(sides):
                    at = span + s * sspan
                    sacc[s, k, GROUP * b : GROUP * b + sspan, lanes(p)] += grad[at : at + sspan]
        return carry

    block_c = slab.shape[3]
    rows_c = width // n_rows
    og = og_ref[...]

    def dp_copy(k, g):
        to = lax.rem(d + k, n_dp)
        at = pl.ds(g * part, part)
        return pltpu.make_async_remote_copy(
            src_ref=slab_low.at[to, :, at], dst_ref=got_dp.at[k - 1, :, at],
            send_sem=dp_sems.at[0, k - 1, g], recv_sem=dp_sems.at[1, k - 1, g],
            device_id={"dp": to}, device_id_type=MESH,
        )

    def cols_copy(k, g):
        to = lax.rem(c + k, n_cols)
        at = pl.ds(g * part, part)
        return pltpu.make_async_remote_copy(
            src_ref=low_cols.at[to, at], dst_ref=got_cols.at[k - 1, at],
            send_sem=cols_sems.at[0, k - 1, g], recv_sem=cols_sems.at[1, k - 1, g],
            device_id={"cols": to}, device_id_type=MESH,
        )

    def rows_copy(to):
        return pltpu.make_async_remote_copy(
            src_ref=low_rows.at[to], dst_ref=got_rows.at[r],
            send_sem=rows_sems.at[0, to], recv_sem=rows_sems.at[1, r],
            device_id={"rows": to}, device_id_type=MESH,
        )

    def rows_arrival(source):
        return pltpu.make_async_remote_copy(
            src_ref=low_rows.at[source], dst_ref=got_rows.at[source],
            send_sem=rows_sems.at[0, source], recv_sem=rows_sems.at[1, source],
            device_id={"rows": source}, device_id_type=MESH,
        )

    def product(g):
        at = slice(g * part, (g + 1) * part)
        left = att_t[at]
        for j in range(n_cols):
            for e in range(n_dp):
                first = (j * n_dp + e) * block_c
                term = mm(left, og[:, first : first + block_c], 1, 0)
                slab[e, j, at] = term
                slab_low[e, j, at] = term.astype(BF16)
        for k in range(1, n_dp):
            dp_copy(k, g).start()

    def sum_dp(g):
        at = slice(g * part, (g + 1) * part)
        for k in range(1, n_dp):
            dp_copy(k, g).wait()
        for j in range(n_cols):
            total = slab[d, j, at]
            for k in range(1, n_dp):
                total = total + got_dp[k - 1, j, at].astype(F32)
            slab[d, j, at] = total
            low_cols[j, at] = total.astype(BF16)
        for k in range(1, n_cols):
            cols_copy(k, g).start()

    def sum_cols(g):
        at = slice(g * part, (g + 1) * part)
        for k in range(1, n_cols):
            cols_copy(k, g).wait()
        total = slab[d, c, at]
        for k in range(1, n_cols):
            total = total + got_cols[k - 1, at].astype(F32)
        slab[d, c, at] = total
        for i in range(part // rows_c):
            to = g * part // rows_c + i
            low_rows[to] = total[i * rows_c : (i + 1) * rows_c].astype(BF16)
            pl.when(r != to)(lambda to=to: rows_copy(to).start())

    def send_rims(g):
        at = slice(g * part, (g + 1) * part)
        for k in range(2):
            rim_out[0, k, :, at] = acc[k, :edge, at].astype(BF16)
            rim_out[1, k, :, at] = acc[k, edge + tokens :, at].astype(BF16)
            for s in range(sides):
                srim_out[s, k, :, at] = sacc[s, k, :, at].astype(BF16)
        start_all(rim_copy, g, rim_send, rim_recv)

    scatters = [scatter(s) for s in range(sides)]

    def add_rims(g):
        at = slice(g * part, (g + 1) * part)
        wait_all(rim_copy, g, rim_send, rim_recv)
        for k in range(2):
            own = acc[k, edge : edge + tokens, at]
            for s in range(sides):
                own = own + mm(scatters[s], srim_in[s, k, :, at], 1, 0)
            acc[k, edge : edge + tokens, at] = own
            acc[k, edge : 2 * edge, at] += rim_in[0, k, :, at].astype(F32)
            acc[k, tokens : edge + tokens, at] += rim_in[1, k, :, at].astype(F32)
            kvg_ref[k, :, at] = acc[k, edge : edge + tokens, at].astype(BF16)

    for g in range(chunks):
        wait_all(halo_copy, g, halo_send, halo_recv)
        lax.fori_loop(g * CHUNK, (g + 1) * CHUNK, attend, 0)
        send_rims(g)
        product(g)
        if g >= 1:
            sum_dp(g - 1)
        if g >= 2:
            sum_cols(g - 2)
    out_ref[...] = mm(att_t[...], w_ref[...], 0, 0).astype(BF16)
    sum_dp(chunks - 1)
    if chunks >= 2:
        sum_cols(chunks - 2)
    for g in range(chunks - 1):
        add_rims(g)
    sum_cols(chunks - 1)
    add_rims(chunks - 1)

    for source in range(n_rows):
        def finish(source=source):
            rows_arrival(source).wait_recv()
            rows_copy(source).wait_send()
        pl.when(r != source)(finish)
    total = slab[d, c, pl.ds(pl.multiple_of(r * rows_c, rows_c), rows_c)]
    for source in range(n_rows):
        total = total + got_rows[source].astype(F32)
    wg_ref[...] = total * (1.0 / math.sqrt(image_h * image_w * n_dp))


def local(n_rows, n_cols, n_dp, queries, keys_values, out_weight, out_grad):
    tile_h, tile_w, width = queries.shape[1:]
    tokens = tile_h * tile_w
    sides = 1 if n_cols == 2 else 2
    blocks = tile_h // QB
    pairs = width // PAIR
    edge = RAD * tile_w
    grown = tokens + 2 * edge
    sgrown = GROUP * (blocks + 2)
    seen = (QB + 2 * RAD) * tile_w + sides * 3 * GROUP
    step = QB * tile_w
    block_c = width // (n_cols * n_dp)
    rows_c = width // n_rows
    links = 2 + 3 * sides
    chunks = pairs // CHUNK
    vmem = pl.BlockSpec(memory_space=pltpu.VMEM)
    dma = pltpu.SemaphoreType.DMA
    out, dq, kvg, wg = pl.pallas_call(
        functools.partial(kernel, tile_h, tile_w, n_rows, n_cols, n_dp),
        out_shape=(
            jax.ShapeDtypeStruct((tokens, width), BF16),
            jax.ShapeDtypeStruct((tokens, width), BF16),
            jax.ShapeDtypeStruct((2, tokens, width), BF16),
            jax.ShapeDtypeStruct((rows_c, block_c), F32),
        ),
        in_specs=[vmem] * 4,
        out_specs=(vmem,) * 4,
        scratch_shapes=[
            pltpu.VMEM((2, grown, width), BF16),
            pltpu.VMEM((sides, 2, sgrown, width), BF16),
            pltpu.VMEM((sides, 2, tile_h * RAD, width), BF16),
            pltpu.VMEM((2, grown, width), F32),
            pltpu.VMEM((sides, 2, sgrown, width), F32),
            pltpu.VMEM((blocks, seen, step), F32),
            pltpu.VMEM((width, tokens), BF16),
            pltpu.VMEM((tokens, width), BF16),
            pltpu.VMEM((2, 2, edge, width), BF16),
            pltpu.VMEM((2, 2, edge, width), BF16),
            pltpu.VMEM((sides, 2, sgrown, width), BF16),
            pltpu.VMEM((sides, 2, sgrown, width), BF16),
            pltpu.VMEM((n_dp, n_cols, width, block_c), F32),
            pltpu.VMEM((n_dp, n_cols, width, block_c), BF16),
            pltpu.VMEM((n_dp - 1, n_cols, width, block_c), BF16),
            pltpu.VMEM((n_cols, width, block_c), BF16),
            pltpu.VMEM((n_cols - 1, width, block_c), BF16),
            pltpu.VMEM((n_rows, rows_c, block_c), BF16),
            pltpu.VMEM((n_rows, rows_c, block_c), BF16),
            dma((links, chunks)), dma((links, chunks)), dma((links, chunks)), dma((links, chunks)),
            dma((2, n_dp - 1, chunks)), dma((2, n_cols - 1, chunks)), dma((2, n_rows)),
        ],
        compiler_params=pltpu.CompilerParams(
            collective_id=0, has_side_effects=True, vmem_limit_bytes=60 * 2**20
        ),
    )(
        queries.reshape(tokens, width),
        keys_values.reshape(2, tokens, width),
        out_weight,
        out_grad.reshape(tokens, width),
    )
    return (
        out.reshape(queries.shape),
        dq.reshape(queries.shape),
        kvg.reshape(keys_values.shape),
        wg,
    )


def solution(mesh):
    in_specs = (
        P("dp", "rows", "cols", None),
        P(None, "dp", "rows", "cols", None),
        P(),
        P("dp", "rows", "cols", None),
    )
    out_specs = (
        P("dp", "rows", "cols", None),
        P("dp", "rows", "cols", None),
        P(None, "dp", "rows", "cols", None),
        P("rows", ("cols", "dp")),
    )
    sizes = (mesh.shape["rows"], mesh.shape["cols"], mesh.shape["dp"])
    return jax.shard_map(
        functools.partial(local, *sizes),
        mesh=mesh, in_specs=in_specs, out_specs=out_specs, check_vma=False,
    )
```

time: 95 us -> 78.3 us (0.82)
  the two profiles are of different devices: /device:TPU:8 before, /device:TPU:28 now
where the time goes in v1:
time: 78.3 us; the launch traced here: 77.8 us
  Pallas kernels  71.6 us (91%)
  local copies, waits for them, and re-layouts  5.49 us (7%)
    pallas_call x1, Pallas kernels, local(): pl.pallas_call(functools.partial(kernel, tile_h, tile_w, n_rows, n_cols,...  71.6 us
    unnamed x8, local copies, waits for them, and re-layouts  5.49 us

profile of v1, /device:TPU:28, one launch (start us, length us, event | category | flops | bytes accessed | tf_op | source)
XLA Modules:
  0.0 77.8 jit_solution(4015168900707531540)
XLA Ops:
  0.6 71.6 %shard_map.75 = (bf16[256,1024]{1,0:T(8,128)(2,1)}, bf16[256,1024]{1,0:T(8,128)(2,1)}, bf16[2,256,1024]{2,1,0:T(8,128)(2,1)}, f32[128,256]{1,0:T(8,128)}) custom-call(bf16[256,1024]{1,0:T(8,128)(2,1)} %bitcast.12, bf16[2,256,1024]{2,1,0:T(8,128)(2,1)} %bitcast.9, bf16[1024,1024]{1,0:T(8,128)(2,1)} %w_ref.1, bf16[256,1024]{1,0:T(8,128)(2,1)} %bitcast.13), custom_call_target="tpu_custom_call" | custom-call | tf_op jit(solution)/shard_map/pallas_call | solution.py:422
  72.3 0.0 copy-start
  72.3 0.0 copy-start.1
  72.3 2.0 %copy.13 = bf16[1,16,16,1024]{3,2,1,0:T(8,128)(2,1)} copy(bf16[1,16,16,1024]{3,2,1,0:T(8,128)(2,1)} %bitcast.11) | data formatting | bytes 1048576
  74.3 1.9 %copy.14 = bf16[1,16,16,1024]{3,2,1,0:T(8,128)(2,1)} copy(bf16[1,16,16,1024]{3,2,1,0:T(8,128)(2,1)} %bitcast.10) | data formatting | bytes 1048576
  76.1 0.0 copy-done
  76.1 1.0 %copy.15 = bf16[2,1,16,16,1024]{4,3,2,1,0:T(8,128)(2,1)} copy(bf16[2,1,16,16,1024]{4,3,2,1,0:T(8,128)(2,1)S(1)} %bitcast.8) | data formatting | bytes 2097152
  77.1 0.0 copy-done.1
  77.1 0.7 copy.16
Async XLA Ops:
  72.3 3.9 %copy-start = (bf16[2,256,1024]{2,1,0:T(8,128)(2,1)S(1)}, bf16[2,256,1024]{2,1,0:T(8,128)(2,1)}, u32[]{:S(2)}) copy-start(bf16[2,256,1024]{2,1,0:T(8,128)(2,1)} %get-tuple-element.10) | copy-start | bytes 3145732
  72.3 4.8 %copy-start.1 = (f32[128,256]{1,0:T(8,128)S(1)}, f32[128,256]{1,0:T(8,128)}, u32[]{:S(2)}) copy-start(f32[128,256]{1,0:T(8,128)} %get-tuple-element.23) | copy-start | bytes 393220

commit v2 on v1

--- a/solution.py
+++ b/solution.py
@@ -14,7 +14,7 @@
 WIN = 13
 QB = 8
 PAIR = 2 * HD
-CHUNK = 2
+CHUNK = 1
 GROUP = QB * RAD
 MESH = pl.DeviceIdType.MESH
 F32 = jnp.float32

time: 78.3 us -> 76.2 us (0.973)
  Pallas kernels: 71.6 us -> 69.8 us
    pallas_call x1, Pallas kernels: 71.6 us -> 69.8 us  [local(): pl.pallas_call(functools.partial(kernel, tile_h, tile_w, n_rows, n_cols,...]
where the time goes in v2:
time: 76.2 us; the launch traced here: 76 us
  Pallas kernels  69.8 us (92%)
  local copies, waits for them, and re-layouts  5.49 us (7%)
    pallas_call x1, Pallas kernels, local(): pl.pallas_call(functools.partial(kernel, tile_h, tile_w, n_rows, n_cols,...  69.8 us
    unnamed x8, local copies, waits for them, and re-layouts  5.49 us

profile of v2, /device:TPU:28, one launch (start us, length us, event | category | flops | bytes accessed | tf_op | source)
XLA Modules:
  0.0 76.0 jit_solution(3688408311195108691)
XLA Ops:
  0.6 69.8 %shard_map.75 = (bf16[256,1024]{1,0:T(8,128)(2,1)}, bf16[256,1024]{1,0:T(8,128)(2,1)}, bf16[2,256,1024]{2,1,0:T(8,128)(2,1)}, f32[128,256]{1,0:T(8,128)}) custom-call(bf16[256,1024]{1,0:T(8,128)(2,1)} %bitcast.12, bf16[2,256,1024]{2,1,0:T(8,128)(2,1)} %bitcast.9, bf16[1024,1024]{1,0:T(8,128)(2,1)} %w_ref.1, bf16[256,1024]{1,0:T(8,128)(2,1)} %bitcast.13), custom_call_target="tpu_custom_call" | custom-call | tf_op jit(solution)/shard_map/pallas_call | solution.py:422
  70.5 0.0 copy-start
  70.5 0.0 copy-start.1
  70.5 2.0 %copy.13 = bf16[1,16,16,1024]{3,2,1,0:T(8,128)(2,1)} copy(bf16[1,16,16,1024]{3,2,1,0:T(8,128)(2,1)} %bitcast.11) | data formatting | bytes 1048576
  72.5 1.9 %copy.14 = bf16[1,16,16,1024]{3,2,1,0:T(8,128)(2,1)} copy(bf16[1,16,16,1024]{3,2,1,0:T(8,128)(2,1)} %bitcast.10) | data formatting | bytes 1048576
  74.3 0.0 copy-done
  74.3 1.0 %copy.15 = bf16[2,1,16,16,1024]{4,3,2,1,0:T(8,128)(2,1)} copy(bf16[2,1,16,16,1024]{4,3,2,1,0:T(8,128)(2,1)S(1)} %bitcast.8) | data formatting | bytes 2097152
  75.3 0.0 copy-done.1
  75.3 0.7 copy.16
Async XLA Ops:
  70.5 3.9 %copy-start = (bf16[2,256,1024]{2,1,0:T(8,128)(2,1)S(1)}, bf16[2,256,1024]{2,1,0:T(8,128)(2,1)}, u32[]{:S(2)}) copy-start(bf16[2,256,1024]{2,1,0:T(8,128)(2,1)} %get-tuple-element.10) | copy-start | bytes 3145732
  70.5 4.8 %copy-start.1 = (f32[128,256]{1,0:T(8,128)S(1)}, f32[128,256]{1,0:T(8,128)}, u32[]{:S(2)}) copy-start(f32[128,256]{1,0:T(8,128)} %get-tuple-element.23) | copy-start | bytes 393220
